TPU v7x, 32 devices: a whole 2x2x4 slice. The times are simulated.
32 devices in a mesh: seq: 8 (over z, y), dp: 4 (over x, core).
Axes of the slice: x: 2, y: 2, z: 4, core: 2. Of those that a mesh axis runs over, the one named last changes fastest.
Arguments:
- out_grad: bfloat16 [4, 1536, 4096], P('dp', 'seq'), may hold values from -6 to 6
- w_out: bfloat16 [2048, 4096], P('dp'), may hold values from -0.125 to 0.125
- queries: bfloat16 [4, 1536, 2048], P('dp', 'seq'), may hold values from -6 to 6
- keys: bfloat16 [4, 1536, 2048], P('dp', 'seq'), may hold values from -6 to 6
- values: bfloat16 [4, 1536, 2048], P('dp', 'seq'), may hold values from -6 to 6
- keep_bits: int32 [4, 1536, 128], P('dp', 'seq'), may hold values from 0 to 65535
- query_later: float32 [4, 16, 128, 128], P('dp'), may hold values from -1.8 to 1.8
Outputs:
- query_grad: bfloat16 [4, 1536, 2048], P('dp', 'seq')
- key_grad: bfloat16 [4, 1536, 2048], P('dp', 'seq')
- value_grad: bfloat16 [4, 1536, 2048], P('dp', 'seq')
All inputs are finite; a program needn't handle non-finite values.
Results may differ from a plain program's by a relative error of at most 0.0058.
Values may be sent and summed in bfloat16 or wider, within the bound.
A program may use at most 192 MiB of HBM per device.

v0:
```python
import jax
import jax.numpy as jnp
from jax import lax
from jax.sharding import PartitionSpec as P

HD = 128


def carried_in(part, axis, combine, identity, reverse):
    count = lax.axis_size(axis)
    place = lax.axis_index(axis)
    ahead = count - 1 - place if reverse else place
    gathered = lax.all_gather(part, axis)
    state = jnp.zeros_like(part) + jnp.asarray(identity, part.dtype)

    def one(step, state):
        source = count - 1 - step if reverse else step
        return combine(state, lax.dynamic_index_in_dim(gathered, source, 0, False))

    return lax.fori_loop(0, ahead, one, state)


def unpack_flags(word_bits, count):
    bit_shift = jnp.arange(16, dtype=jnp.int32)
    flags = word_bits[..., None] >> bit_shift & 1
    return flags.reshape(word_bits.shape[:-1] + (count,)).astype(jnp.float32)


def add_states(earlier, later):
    return earlier + later


def body(out_grad, w_out, queries, keys, values, keep_bits, query_later):
    tok_count = out_grad.shape[1]
    inner_width = queries.shape[2]
    head_size = HD
    head_count = inner_width // head_size
    grad_tokens = out_grad[0]
    projected = lax.dot_general(
        grad_tokens,
        lax.all_gather(w_out, "dp", axis=0, tiled=True),
        (((1,), (1,)), ((), ())),
        preferred_element_type=jnp.float32,
    )
    keep_mask = unpack_flags(keep_bits[0], inner_width)
    position = (lax.axis_index("seq") * tok_count + jnp.arange(tok_count, dtype=jnp.int32)).astype(
        jnp.float32
    )
    row_scale = 2.0 / jnp.sqrt(head_size * (position + 1.0))
    gated = (projected * keep_mask * row_scale[:, None]).astype(jnp.bfloat16)
    gated_heads = gated.reshape(tok_count, head_count, head_size)
    query_heads = queries[0].reshape(tok_count, head_count, head_size)
    key_heads = keys[0].reshape(tok_count, head_count, head_size)
    value_heads = values[0].reshape(tok_count, head_count, head_size)
    key_state = jnp.einsum(
        "thi,thj->hij", key_heads, value_heads, preferred_element_type=jnp.float32
    )
    query_state = jnp.einsum(
        "thi,thj->hij", query_heads, gated_heads, preferred_element_type=jnp.float32
    )
    zero_state = jnp.zeros_like(key_state)
    key_before = carried_in(key_state, "seq", add_states, zero_state, False)
    query_after = carried_in(query_state, "seq", add_states, zero_state, True)
    query_after = query_after + query_later[0]
    key_before_b = key_before.astype(jnp.bfloat16)
    query_after_b = query_after.astype(jnp.bfloat16)
    causal_mask = (jnp.arange(tok_count)[:, None] >= jnp.arange(tok_count)[None, :]).astype(
        jnp.float32
    )
    grad_scores = (
        jnp.einsum("thj,shj->hts", gated_heads, value_heads, preferred_element_type=jnp.float32)
        * causal_mask
    ).astype(jnp.bfloat16)
    attn_scores = (
        jnp.einsum("thj,shj->hts", query_heads, key_heads, preferred_element_type=jnp.float32)
        * causal_mask
    ).astype(jnp.bfloat16)
    query_grad = jnp.einsum(
        "hts,shi->thi", grad_scores, key_heads, preferred_element_type=jnp.float32
    )
    query_grad = query_grad + jnp.einsum(
        "thj,hij->thi", gated_heads, key_before_b, preferred_element_type=jnp.float32
    )
    key_grad = jnp.einsum(
        "hts,thi->shi", grad_scores, query_heads, preferred_element_type=jnp.float32
    )
    key_grad = key_grad + jnp.einsum(
        "shj,hij->shi", value_heads, query_after_b, preferred_element_type=jnp.float32
    )
    value_grad = jnp.einsum(
        "hts,thj->shj", attn_scores, gated_heads, preferred_element_type=jnp.float32
    )
    value_grad = value_grad + jnp.einsum(
        "shi,hij->shj", key_heads, query_after_b, preferred_element_type=jnp.float32
    )

    def merge_heads(tensor):
        return tensor.reshape(1, tok_count, inner_width).astype(jnp.bfloat16)

    return (merge_heads(query_grad), merge_heads(key_grad), merge_heads(value_grad))


def solution(mesh):
    in_specs = (
        P("dp", "seq", None),
        P("dp", None),
        P("dp", "seq", None),
        P("dp", "seq", None),
        P("dp", "seq", None),
        P("dp", "seq", None),
        P("dp", None, None, None),
    )
    out_specs = (P("dp", "seq", None), P("dp", "seq", None), P("dp", "seq", None))
    return jax.shard_map(body, mesh=mesh, in_specs=in_specs, out_specs=out_specs, check_vma=False)
```

profile of v0, /device:TPU:0, one launch (start us, length us, event | category | flops | bytes accessed | tf_op | source)
XLA Modules:
  0.0 395.9 jit_solution(10310405240292140329)
XLA Ops:
  7.2 0.0 all-gather.6.cloned.1.call-start
  7.2 0.7 all-gather.6.cloned.1.call-update
  7.9 0.0 all-gather.8.cloned.1.call-start
  8.0 0.5 copy-done.10
  8.4 0.2 copy.71
  8.6 0.6 copy-done.11
  9.2 0.2 copy.70
  9.3 1.5 fusion.21
  10.9 0.0 all-gather.8.cloned.1.call-update
  10.9 0.0 all-gather.10.cloned.1.call-start
  11.0 0.1 copy.45
  11.1 1.6 shift_right_arithmetic.23
  12.6 2.9 copy.46
  15.6 0.1 shift_right_arithmetic.26
  15.6 1.2 copy.72
  16.8 101.4 %all-gather.6.cloned.1.call-done = bf16[2048,4096]{1,0:T(8,128)(2,1)} async-done(((bf16[512,4096]{1,0:T(8,128)(2,1)}), bf16[2048,4096]{1,0:T(8,128)(2,1)}) %all-gather.6.cloned.1.call-update) | async-done | bytes 16777232 | tf_op jit(solution)/shard_map/all_gather | solution.py:41
  118.2 11.9 %fusion.7 = bf16[24,16,8,128]{3,2,1,0:T(8,128)(2,1)S(1)} fusion(s32[192,2048]{1,0:T(8,128)} %copy.46, bf16[2048,4096]{1,0:T(8,128)(2,1)} %all-gather.6.cloned.1.call-done, bf16[1,192,4096]{2,1,0:T(8,128)(2,1)S(1)} %copy-done, f32[192]{0:T(256)S(1)} %rsqrt_multiply_fusion, s32[2048]{0:T(1024)S(1)} %shift_right_arithmetic.26), kind=kOutput, calls=%fused_computation.16 | convolution fusion | flops 3223584768 | bytes 20718336 | tf_op jit(solution)/shard_map/dot_general | solution.py:39
  130.2 1.9 convolution_bitcast_fusion
  132.1 1.3 copy.58
  133.5 0.7 fusion.35
  134.2 111.2 %all-gather.8.cloned.1.call-done = f32[128,128,128]{2,1,0:T(8,128)} async-done(((f32[16,128,128]{2,1,0:T(8,128)}), f32[128,128,128]{2,1,0:T(8,128)}) %all-gather.8.cloned.1.call-update) | async-done | bytes 8388624 | tf_op jit(solution)/shard_map/all_gather | solution.py:13
  245.3 0.1 broadcast_in_dim.2.clone
  245.5 1.8 multiply_convert_fusion.1
  247.3 0.6 fusion.33
  247.9 0.6 copy-done.7
  248.5 0.5 fusion.3
  249.0 0.5 copy.53
  249.5 1.2 convert_element_type.86
  250.7 3.2 fusion.18
  253.9 3.7 fusion.5
  257.6 113.0 %all-gather.10.cloned.1.call-done = f32[128,128,128]{2,1,0:T(8,128)} async-done(((f32[16,128,128]{2,1,0:T(8,128)}), f32[128,128,128]{2,1,0:T(8,128)}) %all-gather.10.cloned.1.call-update) | async-done | bytes 8388624 | tf_op jit(solution)/shard_map/all_gather | solution.py:13
  370.6 0.1 broadcast_in_dim.2.clone.1
  370.7 10.8 %while.23 = (s32[]{:T(128)}, f32[16,128,128]{2,1,0:T(8,128)S(1)}, s32[]{:T(128)}, f32[8,16,128,128]{3,2,1,0:T(8,128)}, s32[]{:T(128)}, /*index=5*/s32[]{:T(128)}, s32[]{:T(128)}, s32[]{:T(128)}) while((s32[]{:T(128)}, f32[16,128,128]{2,1,0:T(8,128)S(1)}, s32[]{:T(128)}, f32[8,16,128,128]{3,2,1,0:T(8,128)}, s32[]{:T(128)}, ...), condition=%wide.region_3.4_spmd, body=%wide.region_2.3_spmd.sunk | while | flops 262150 | bytes 3145863 | solution.py:20
  370.7 1.5 bitcast_add_fusion.8
  372.3 1.5 bitcast_add_fusion.8
  373.8 1.5 bitcast_add_fusion.8
  375.3 1.5 bitcast_add_fusion.8
  376.8 1.5 bitcast_add_fusion.8
  378.3 1.5 bitcast_add_fusion.8
  379.8 1.5 bitcast_add_fusion.8
  381.5 1.5 fusion.10
  383.1 0.4 copy-done.8
  383.5 0.4 fusion.6
  383.9 0.5 copy.66
  384.4 1.2 convert_element_type.93
  385.6 2.0 fusion.2
  387.6 0.5 copy.60
  388.1 1.2 convert_element_type.89
  (28 shorter events, 0.1 us)
Async XLA Ops:
  7.2 111.1 %copy-start = (bf16[1,192,4096]{2,1,0:T(8,128)(2,1)S(1)}, bf16[1,192,4096]{2,1,0:T(8,128)(2,1)}, u32[]{:S(2)}) copy-start(bf16[1,192,4096]{2,1,0:T(8,128)(2,1)} %param.11) | copy-start | bytes 4718596
  7.2 1.3 copy-start.10
  7.2 111.0 %all-gather.6.cloned.1.call-start = ((), (), s32[]{:S(2)}) async-start(), calls=%async_computation | async-start | bytes 20971520 | tf_op jit(solution)/shard_map/all_gather | solution.py:41
  7.9 237.4 %all-gather.8.cloned.1.call-start = ((), (), s32[]{:S(2)}) async-start(), calls=%async_computation.1 | async-start | bytes 9437184 | tf_op jit(solution)/shard_map/all_gather | solution.py:13
  8.0 1.2 copy-start.11
  8.6 2.3 copy-start.2
  9.3 1.6 copy-start.13
  10.9 359.7 %all-gather.10.cloned.1.call-start = ((), (), s32[]{:S(2)}) async-start(), calls=%async_computation.2 | async-start | bytes 9437184 | tf_op jit(solution)/shard_map/all_gather | solution.py:13
  12.6 3.0 copy-start.12
  130.2 115.3 %copy-start.6 = (bf16[24,16,8,128]{3,2,1,0:T(8,128)(2,1)}, bf16[24,16,8,128]{3,2,1,0:T(8,128)(2,1)S(1)}, u32[]{:S(2)}) copy-start(bf16[24,16,8,128]{3,2,1,0:T(8,128)(2,1)S(1)} %fusion.7) | copy-start | bytes 2359300
  245.5 1.9 copy-start.3
  247.3 1.1 copy-start.7
  250.7 3.2 copy-start.4
  250.7 3.2 copy-start.9
  381.5 1.5 copy-start.5
  381.5 2.0 copy-start.8
  385.6 3.7 copy-start.1
Sparse Core Ops, SparseCore 0:
  9.6 108.6 all-gather.5
  120.4 124.9 all-gather.7
  247.5 123.1 all-gather.9
where the time goes:
time: 397 us; the launch traced here: 396 us
  waiting for transfers between devices  326 us (82%)
  matrix products  27.6 us (7%)
  local copies, waits for them, and re-layouts  14.9 us (4%)
  between operations  14 us (4%)
  other arithmetic  12.6 us (3%)
    all_gather x2, waiting for transfers between devices, carried_in(): gathered = lax.all_gather(part, axis)  224 us
    all_gather x1, waiting for transfers between devices, body(): lax.all_gather(w_out, 'dp', axis=0, tiled=True)  101 us
    dot_general x1, matrix products, body(): lax.dot_general(grad_tokens, lax.all_gather(w_out, 'dp', axis=0, tiled=Tr...  11.9 us
    add x7, other arithmetic, add_states(): return earlier + later  10.4 us
  transfers between devices with their start and end apart: 3, of which 3 were waited for; matrix products, arithmetic and copies ran while one was open for 9% of the time, Pallas kernels for 0%

commit v1 on v0

v1 whole, which is shorter than its diff:
```python
import functools

import jax
import jax.numpy as jnp
from jax import lax
from jax.experimental import pallas as pl
from jax.experimental.pallas import tpu as pltpu
from jax.sharding import PartitionSpec as P

HD = 128
NC = 4
KT = 1024
FT = 256
MESH = pl.DeviceIdType.MESH
F32 = jnp.float32
BF = jnp.bfloat16


def dot_nt(a, b):
    return lax.dot_general(a, b, (((1,), (1,)), ((), ())), preferred_element_type=F32)


def dot_tn(a, b):
    return lax.dot_general(a, b, (((0,), (0,)), ((), ())), preferred_element_type=F32)


def dot_nn(a, b):
    return lax.dot_general(a, b, (((1,), (0,)), ((), ())), preferred_element_type=F32)


def split(start, count, size):
    return [(start + i, min(size, count - i)) for i in range(0, count, size)]


def kernel(
    n_seq, n_dp,
    og, w, q, k, v, kb, ql,
    qg, kg, vg,
    wbuf, g_own, g_rem, qb, kbuf, vb, kbits, qlb,
    gat, mk, ret, ks, kr, ki, ko, kbf, qs, qr, qi, qo, qaf, kgp, vgp, ob,
    ld, wsem, gsend, grecv, rsend, rrecv, kps, kpr, kcs, kcr, qps, qpr, qcs, qcr, osem,
):
    T, D = g_own.shape
    Wr = wbuf.shape[1]
    Fc = 2 * Wr
    Hc = Fc // HD
    X = n_dp // 2
    H = qb.shape[1] // HD
    R = T // NC
    n = lax.axis_index("seq")
    d = lax.axis_index("dp")
    x = d // 2
    c = lax.rem(d, 2)
    odd = lax.rem(n, 2)
    mate = n + 1 - 2 * odd
    has_lo = n >= 2
    has_hi = n < n_seq - 2
    core = (n, x * 2 + 1 - c)
    far = [(n, lax.rem(x + j, X) * 2 + c) for j in range(1, X)]

    barrier = pltpu.get_barrier_semaphore()
    for peer in [core, (mate, d)] + far:
        pl.semaphore_signal(barrier, inc=1, device_id=peer, device_id_type=MESH)

    @pl.when(has_lo)
    def _():
        pl.semaphore_signal(barrier, inc=1, device_id=(n - 2, d), device_id_type=MESH)

    @pl.when(has_hi)
    def _():
        pl.semaphore_signal(barrier, inc=1, device_id=(n + 2, d), device_id_type=MESH)

    loads = [
        pltpu.make_async_copy(k.at[0], kbuf, ld.at[0]),
        pltpu.make_async_copy(v.at[0], vb, ld.at[1]),
        pltpu.make_async_copy(kb.at[0], kbits, ld.at[2]),
        pltpu.make_async_copy(og.at[0], g_own, ld.at[3]),
        pltpu.make_async_copy(w, wbuf.at[c], ld.at[4]),
        pltpu.make_async_copy(q.at[0], qb, ld.at[5]),
        pltpu.make_async_copy(ql.at[0], qlb, ld.at[6]),
    ]
    for copy in loads:
        copy.start()
    pl.semaphore_wait(
        barrier, 1 + X + has_lo.astype(jnp.int32) + has_hi.astype(jnp.int32)
    )

    def remote(src, dst, ss, rs, dev):
        return pltpu.make_async_remote_copy(
            src_ref=src, dst_ref=dst, send_sem=ss, recv_sem=rs, device_id=dev, device_id_type=MESH
        )

    grad_copies = {}
    for i in range(NC):
        for j in range(1, X):
            s = X - 1 - j
            grad_copies[i, s] = remote(
                og.at[0, pl.ds(i * R, R), :], g_rem.at[s, pl.ds(i * R, R), :],
                gsend.at[i, j - 1], grecv.at[i, s], far[j - 1],
            )
            grad_copies[i, s].start()
    w_copy = remote(w, wbuf.at[c], wsem.at[0], wsem.at[1], core)
    w_copy.start()

    @pl.when(jnp.logical_not(has_lo))
    def _():
        ki[...] = jnp.zeros_like(ki)

    @pl.when(jnp.logical_not(has_hi))
    def _():
        qi[...] = jnp.zeros_like(qi)

    def lanes(h):
        return pl.ds(pl.multiple_of(h * HD, HD), HD)

    def head_of(j, hl):
        return lax.rem(x + j, X) * Hc + hl

    loads[0].wait()
    loads[1].wait()
    key_groups = split(0, H, 4)
    key_pair = []
    for gi, (p0, cnt) in enumerate(key_groups):
        @pl.loop(0, cnt)
        def _(i):
            h = p0 + i
            ks[h] = dot_tn(kbuf[:, lanes(h)], vb[:, lanes(h)]).astype(BF)

        copy = remote(ks.at[pl.ds(p0, cnt)], kr.at[pl.ds(p0, cnt)], kps.at[gi], kpr.at[gi], (mate, d))
        copy.start()
        key_pair.append(copy)

    loads[2].wait()
    words = kbits.shape[1]
    low = (kbits[...] & 255).astype(F32).astype(BF)
    high = (kbits[...] >> 8).astype(F32).astype(BF)
    row = lax.broadcasted_iota(jnp.int32, (words, HD), 0)
    lane = lax.broadcasted_iota(jnp.int32, (words, HD), 1)
    bit = lax.broadcasted_iota(jnp.int32, (T, HD), 1) & 7

    @pl.loop(0, H)
    def _(h):
        here = row == (lane >> 4) + h * 8
        first = (lane & 15) < 8
        pick_low = jnp.where(here & first, 1.0, 0.0).astype(BF)
        pick_high = jnp.where(here & jnp.logical_not(first), 1.0, 0.0).astype(BF)
        word = (dot_nn(low, pick_low) + dot_nn(high, pick_high)).astype(jnp.int32)
        mk[:, lanes(h)] = ((word >> bit) & 1).astype(F32).astype(BF)

    def project(g_ref, row0, rows, dst):
        pos = (n * T + row0 + lax.broadcasted_iota(jnp.int32, (rows, 1), 0)).astype(F32)
        scale = 2.0 / jnp.sqrt(HD * (pos + 1.0))
        for cc in range(2):
            @pl.loop(0, Wr // FT)
            def _(i):
                off = pl.multiple_of(i * FT, FT)
                acc = jnp.zeros((rows, FT), F32)
                for kk in range(0, D, KT):
                    acc = acc + dot_nt(
                        g_ref[pl.ds(row0, rows), pl.ds(kk, KT)],
                        wbuf[cc, pl.ds(off, FT), pl.ds(kk, KT)],
                    )
                dst[pl.ds(row0, rows), pl.ds(pl.multiple_of(cc * Wr + off, FT), FT)] = (
                    acc * scale
                ).astype(BF)

    def query_states(j, hl0, cnt):
        @pl.loop(0, cnt)
        def _(i):
            hl = hl0 + i
            h = head_of(j, hl)
            g = gat[j, :, lanes(hl)] * mk[:, lanes(h)]
            gat[j, :, lanes(hl)] = g
            qs[j * Hc + hl] = dot_tn(qb[:, lanes(h)], g).astype(BF)

    q_groups = []
    for j in range(X):
        for hl0, cnt in split(0, Hc, 4 if j == 0 else 2):
            q_groups.append((j, hl0, cnt))
    query_pair = {}

    def send_query_states(gi):
        j, hl0, cnt = q_groups[gi]
        query_states(j, hl0, cnt)
        rows = pl.ds(j * Hc + hl0, cnt)
        copy = remote(qs.at[rows], qr.at[rows], qps.at[gi], qpr.at[gi], (mate, d))
        copy.start()
        query_pair[gi] = copy

    def chain(gi, rows, pair, mine, got, inn, out, ss, rs, wait_if, send_if, to):
        pair.wait_recv()
        copy = remote(out.at[rows], inn.at[rows], ss.at[gi], rs.at[gi], to)

        @pl.when(wait_if)
        def _():
            copy.wait_recv()

        @pl.when(send_if)
        def _():
            out[rows] = (
                inn[rows].astype(F32) + (mine[rows].astype(F32) + got[rows].astype(F32))
            ).astype(BF)
            copy.start()

        return copy

    odd_f = odd.astype(F32)
    key_chain = []

    def key_step(gi):
        p0, cnt = key_groups[gi]
        rows = pl.ds(p0, cnt)
        to = (jnp.minimum(n + 2, n_seq - 2 + odd), d)
        key_chain.append(
            chain(gi, rows, key_pair[gi], ks, kr, ki, ko, kcs, kcr, has_lo, has_hi, to)
        )
        kbf[rows] = (ki[rows].astype(F32) + kr[rows].astype(F32) * odd_f).astype(BF)

    query_chain = []

    def query_step(gi):
        j, hl0, cnt = q_groups[gi]
        rows = pl.ds(j * Hc + hl0, cnt)
        to = (jnp.maximum(n - 2, odd), d)
        query_chain.append(
            chain(gi, rows, query_pair[gi], qs, qr, qi, qo, qcs, qcr, has_hi, has_lo, to)
        )

        @pl.loop(0, cnt)
        def _(i):
            p = j * Hc + hl0 + i
            h = head_of(j, hl0 + i)
            qaf[p] = (
                qlb[h] + (qi[p].astype(F32) + qr[p].astype(F32) * (1.0 - odd_f))
            ).astype(BF)

    tri = (
        lax.broadcasted_iota(jnp.int32, (T, T), 0) >= lax.broadcasted_iota(jnp.int32, (T, T), 1)
    )

    def inside(j):
        @pl.loop(0, Hc)
        def _(hl):
            h = head_of(j, hl)
            p = j * Hc + hl
            g = gat[j, :, lanes(hl)]
            qh, kh, vh = qb[:, lanes(h)], kbuf[:, lanes(h)], vb[:, lanes(h)]
            gs = jnp.where(tri, dot_nt(g, vh), 0.0).astype(BF)
            at = jnp.where(tri, dot_nt(qh, kh), 0.0).astype(BF)
            ob[0, :, lanes(h)] = (dot_nn(gs, kh) + dot_nt(g, kbf[h])).astype(BF)
            kgp[p] = dot_tn(gs, qh)
            vgp[p] = dot_tn(at, g)

    def across(j, hl0, cnt):
        @pl.loop(0, cnt)
        def _(i):
            hl = hl0 + i
            h = head_of(j, hl)
            p = j * Hc + hl
            qa = qaf[p]
            ob[1, :, lanes(h)] = (kgp[p] + dot_nt(vb[:, lanes(h)], qa)).astype(BF)
            ob[2, :, lanes(h)] = (vgp[p] + dot_nn(kbuf[:, lanes(h)], qa)).astype(BF)

    outs = []

    def store(o, j):
        cols = pl.ds(pl.multiple_of(lax.rem(x + j, X) * Fc, Fc), Fc)
        copy = pltpu.make_async_copy(
            ob.at[o, :, cols], (qg, kg, vg)[o].at[0, :, cols], osem.at[o, j]
        )
        copy.start()
        outs.append(copy)

    loads[3].wait()
    loads[4].wait()
    w_copy.wait_recv()
    project(g_own, 0, T, gat.at[0])
    loads[5].wait()
    loads[6].wait()
    local = [gi for gi, g in enumerate(q_groups) if g[0] == 0]
    distant = [gi for gi, g in enumerate(q_groups) if g[0] > 0]
    for gi in local:
        send_query_states(gi)
    for gi in range(len(key_groups)):
        key_step(gi)

    ret_copies = []

    def serve(i):
        for s in range(X - 1):
            grad_copies[i, s].wait_recv()
            project(g_rem.at[s], i * R, R, ret.at[s])
            back = X - 1 - s
            copy = remote(
                ret.at[s, pl.ds(i * R, R), :], gat.at[back, pl.ds(i * R, R), :],
                rsend.at[i, s], rrecv.at[i, back - 1], far[s],
            )
            copy.start()
            ret_copies.append(copy)

    serve(0)
    for gi in local:
        query_step(gi)
    inside(0)
    store(0, 0)
    serve(1)
    for gi in local:
        across(*q_groups[gi])
    store(1, 0)
    store(2, 0)
    for i in range(2, NC):
        serve(i)
    for copy in ret_copies:
        copy.wait_recv()
    for gi in distant:
        send_query_states(gi)
    for j in range(1, X):
        inside(j)
        store(0, j)
    for gi in distant:
        query_step(gi)
        across(*q_groups[gi])
    for j in range(1, X):
        store(1, j)
        store(2, j)

    for copy in list(grad_copies.values()) + [w_copy] + ret_copies + key_pair:
        copy.wait_send()
    for copy in query_pair.values():
        copy.wait_send()

    @pl.when(has_hi)
    def _():
        for copy in key_chain:
            copy.wait_send()

    @pl.when(has_lo)
    def _():
        for copy in query_chain:
            copy.wait_send()

    for copy in outs:
        copy.wait()


def body(n_seq, n_dp, out_grad, w_out, queries, keys, values, keep_bits, query_later):
    T, D = out_grad.shape[1:]
    I = queries.shape[2]
    Wr = w_out.shape[0]
    Fc = 2 * Wr
    Hc = Fc // HD
    X = n_dp // 2
    H = I // HD
    kgn = len(split(0, H, 4))
    qgn = len(split(0, Hc, 4)) + (X - 1) * len(split(0, Hc, 2))
    state = pltpu.VMEM((H, HD, HD), BF)
    dma = pltpu.SemaphoreType.DMA
    far = max(X - 1, 1)
    scratch = [
        pltpu.VMEM((2, Wr, D), BF),
        pltpu.VMEM((T, D), BF),
        pltpu.VMEM((far, T, D), BF),
        pltpu.VMEM((T, I), BF),
        pltpu.VMEM((T, I), BF),
        pltpu.VMEM((T, I), BF),
        pltpu.VMEM((T, keep_bits.shape[2]), jnp.int32),
        pltpu.VMEM((H, HD, HD), F32),
        pltpu.VMEM((X, T, Fc), BF),
        pltpu.VMEM((T, I), BF),
        pltpu.VMEM((far, T, Fc), BF),
        state, state, state, state, state,
        state, state, state, state, state,
        pltpu.VMEM((H, T, HD), F32),
        pltpu.VMEM((H, T, HD), F32),
        pltpu.VMEM((3, T, I), BF),
        dma((7,)), dma((2,)),
        dma((NC, far)), dma((NC, far)), dma((NC, far)), dma((NC, far)),
        dma((kgn,)), dma((kgn,)), dma((kgn,)), dma((kgn,)),
        dma((qgn,)), dma((qgn,)), dma((qgn,)), dma((qgn,)),
        dma((3, X)),
    ]
    out = jax.ShapeDtypeStruct((1, T, I), BF)
    hbm = pl.BlockSpec(memory_space=pl.ANY)
    return pl.pallas_call(
        functools.partial(kernel, n_seq, n_dp),
        out_shape=(out, out, out),
        in_specs=[hbm] * 7,
        out_specs=(hbm, hbm, hbm),
        scratch_shapes=scratch,
        compiler_params=pltpu.CompilerParams(
            collective_id=0, has_side_effects=True, vmem_limit_bytes=60 * 1024 * 1024
        ),
    )(out_grad, w_out, queries, keys, values, keep_bits, query_later)


def solution(mesh):
    rows = P("dp", "seq", None)
    in_specs = (rows, P("dp", None), rows, rows, rows, rows, P("dp", None, None, None))
    fn = functools.partial(body, mesh.shape["seq"], mesh.shape["dp"])
    return jax.shard_map(fn, mesh=mesh, in_specs=in_specs, out_specs=(rows, rows, rows), check_vma=False)
```

time: 397 us -> 92.6 us (0.23)
  waiting for transfers between devices: 326 us -> 0 us
  Pallas kernels: 0 us -> 85.5 us
  matrix products: 27.6 us -> 0 us
  between operations: 14 us -> 0.64 us
  other arithmetic: 12.6 us -> 0 us
  local copies, waits for them, and re-layouts: 14.9 us -> 6.26 us
    all_gather x3 -> x0, waiting for transfers between devices: 326 us -> none  [the longest x2 224 us: carried_in(): gathered = lax.all_gather(part, axis)]
    pallas_call x0 -> x1, Pallas kernels: none -> 85.5 us  [body(): pl.pallas_call(functools.partial(kernel, n_seq, n_dp), out_shape=(out, ou...]
    dot_general x10 -> x0, matrix products: 27.6 us -> none  [the longest x1 11.9 us: body(): lax.dot_general(grad_tokens, lax.all_gather(w_out, 'dp', axis=0, tiled=Tr...]
    add x7 -> x0, other arithmetic: 10.4 us -> none  [add_states(): return earlier + later]
    convert_element_type x6 -> x0, local copies, waits for them, and re-layouts: 5.17 us -> none  [merge_heads(): return tensor.reshape(1, tok_count, inner_width).astype(jnp.bfloat16)]
    shift_right_arithmetic x5 -> x0, local copies, waits for them, and re-layouts: 4.64 us -> none  [unpack_flags(): flags = word_bits[..., None] >> bit_shift & 1]
  transfers between devices with their start and end apart: 3 -> 0, of which waited for: 3 -> 0; matrix products, arithmetic and copies ran while one was open for 9% -> 0% of each run, Pallas kernels for 0% -> 0%
where the time goes in v1:
time: 92.6 us; the launch traced here: 92.4 us
  Pallas kernels  85.5 us (92%)
  local copies, waits for them, and re-layouts  6.26 us (7%)
    pallas_call x1, Pallas kernels, body(): pl.pallas_call(functools.partial(kernel, n_seq, n_dp), out_shape=(out, ou...  85.5 us
    unnamed x3, local copies, waits for them, and re-layouts  6.26 us

profile of v1, /device:TPU:0, one launch (start us, length us, event | category | flops | bytes accessed | tf_op | source)
XLA Modules:
  0.0 92.4 jit_solution(630967643716862413)
XLA Ops:
  0.6 85.5 %shard_map.94 = (bf16[1,192,2048]{2,1,0:T(8,128)(2,1)}, bf16[1,192,2048]{2,1,0:T(8,128)(2,1)}, bf16[1,192,2048]{2,1,0:T(8,128)(2,1)}) custom-call(bf16[1,192,4096]{2,1,0:T(8,128)(2,1)} %og.1, bf16[512,4096]{1,0:T(8,128)(2,1)} %w.1, bf16[1,192,2048]{2,1,0:T(8,128)(2,1)} %q.1, bf16[1,192,2048]{2,1,0:T(8,128)(2,1)} %k.1, bf16[1,192,2048]{2,1,0:T(8,128)(2,1)} %v.1, ...), custom_call_target="tpu_custom_call" | custom-call | tf_op jit(solution)/shard_map/pallas_call | solution.py:384
  86.1 2.1 %copy.13 = bf16[1,192,2048]{2,1,0:T(8,128)(2,1)} copy(bf16[1,192,2048]{2,1,0:T(8,128)(2,1)} %get-tuple-element.6) | data formatting | bytes 1572864
  88.2 2.1 %copy.14 = bf16[1,192,2048]{2,1,0:T(8,128)(2,1)} copy(bf16[1,192,2048]{2,1,0:T(8,128)(2,1)} %get-tuple-element.7) | data formatting | bytes 1572864
  90.3 2.1 %copy.15 = bf16[1,192,2048]{2,1,0:T(8,128)(2,1)} copy(bf16[1,192,2048]{2,1,0:T(8,128)(2,1)} %get-tuple-element.8) | data formatting | bytes 1572864

commit v2 on v1

--- a/solution.py
+++ b/solution.py
@@ -37,7 +37,7 @@
     og, w, q, k, v, kb, ql,
     qg, kg, vg,
     wbuf, g_own, g_rem, qb, kbuf, vb, kbits, qlb,
-    gat, mk, ret, ks, kr, ki, ko, kbf, qs, qr, qi, qo, qaf, kgp, vgp, ob,
+    gat, mk, ret, ks, kr, ki, ko, kbf, qs, qr, qi, qo, qaf, qgp, kgp, vgp, ob,
     ld, wsem, gsend, grecv, rsend, rrecv, kps, kpr, kcs, kcr, qps, qpr, qcs, qcr, osem,
 ):
     T, D = g_own.shape
@@ -53,6 +53,8 @@
     c = lax.rem(d, 2)
     odd = lax.rem(n, 2)
     mate = n + 1 - 2 * odd
+    level = n // 2
+    back_level = n_seq // 2 - 1 - level
     has_lo = n >= 2
     has_hi = n < n_seq - 2
     core = (n, x * 2 + 1 - c)
@@ -147,10 +149,10 @@
         word = (dot_nn(low, pick_low) + dot_nn(high, pick_high)).astype(jnp.int32)
         mk[:, lanes(h)] = ((word >> bit) & 1).astype(F32).astype(BF)
 
-    def project(g_ref, row0, rows, dst):
+    def project(g_ref, row0, rows, dst, halves):
         pos = (n * T + row0 + lax.broadcasted_iota(jnp.int32, (rows, 1), 0)).astype(F32)
         scale = 2.0 / jnp.sqrt(HD * (pos + 1.0))
-        for cc in range(2):
+        for cc in halves:
             @pl.loop(0, Wr // FT)
             def _(i):
                 off = pl.multiple_of(i * FT, FT)
@@ -187,9 +189,8 @@
         copy.start()
         query_pair[gi] = copy
 
-    def chain(gi, rows, pair, mine, got, inn, out, ss, rs, wait_if, send_if, to):
+    def chain(rows, copy, pair, mine, got, inn, out, wait_if, send_if):
         pair.wait_recv()
-        copy = remote(out.at[rows], inn.at[rows], ss.at[gi], rs.at[gi], to)
 
         @pl.when(wait_if)
         def _():
@@ -202,29 +203,29 @@
             ).astype(BF)
             copy.start()
 
-        return copy
-
     odd_f = odd.astype(F32)
-    key_chain = []
-
-    def key_step(gi):
+
+    def key_copy(gi):
         p0, cnt = key_groups[gi]
         rows = pl.ds(p0, cnt)
         to = (jnp.minimum(n + 2, n_seq - 2 + odd), d)
-        key_chain.append(
-            chain(gi, rows, key_pair[gi], ks, kr, ki, ko, kcs, kcr, has_lo, has_hi, to)
-        )
-        kbf[rows] = (ki[rows].astype(F32) + kr[rows].astype(F32) * odd_f).astype(BF)
-
-    query_chain = []
-
-    def query_step(gi):
+        return rows, remote(ko.at[rows], ki.at[rows], kcs.at[gi], kcr.at[gi], to)
+
+    def query_copy(gi):
         j, hl0, cnt = q_groups[gi]
         rows = pl.ds(j * Hc + hl0, cnt)
         to = (jnp.maximum(n - 2, odd), d)
-        query_chain.append(
-            chain(gi, rows, query_pair[gi], qs, qr, qi, qo, qcs, qcr, has_hi, has_lo, to)
-        )
+        return rows, remote(qo.at[rows], qi.at[rows], qcs.at[gi], qcr.at[gi], to)
+
+    def key_step(gi):
+        rows, copy = key_copy(gi)
+        chain(rows, copy, key_pair[gi], ks, kr, ki, ko, has_lo, has_hi)
+        kbf[rows] = (ki[rows].astype(F32) + kr[rows].astype(F32) * odd_f).astype(BF)
+
+    def query_step(gi):
+        rows, copy = query_copy(gi)
+        chain(rows, copy, query_pair[gi], qs, qr, qi, qo, has_hi, has_lo)
+        j, hl0, cnt = q_groups[gi]
 
         @pl.loop(0, cnt)
         def _(i):
@@ -247,11 +248,20 @@
             qh, kh, vh = qb[:, lanes(h)], kbuf[:, lanes(h)], vb[:, lanes(h)]
             gs = jnp.where(tri, dot_nt(g, vh), 0.0).astype(BF)
             at = jnp.where(tri, dot_nt(qh, kh), 0.0).astype(BF)
-            ob[0, :, lanes(h)] = (dot_nn(gs, kh) + dot_nt(g, kbf[h])).astype(BF)
+            qgp[p] = dot_nn(gs, kh)
             kgp[p] = dot_tn(gs, qh)
             vgp[p] = dot_tn(at, g)
 
-    def across(j, hl0, cnt):
+    def across_k():
+        for j in range(X):
+            @pl.loop(0, Hc)
+            def _(hl):
+                h = head_of(j, hl)
+                ob[0, :, lanes(h)] = (
+                    qgp[j * Hc + hl] + dot_nt(gat[j, :, lanes(hl)], kbf[h])
+                ).astype(BF)
+
+    def across_q(j, hl0, cnt):
         @pl.loop(0, cnt)
         def _(i):
             hl = hl0 + i
@@ -271,25 +281,41 @@
         copy.start()
         outs.append(copy)
 
+    local = [gi for gi, g in enumerate(q_groups) if g[0] == 0]
+    distant = [gi for gi, g in enumerate(q_groups) if g[0] > 0]
+
+    def slot(place, number):
+        return place >= number if number == 3 else place == number
+
+    def key_slot(number):
+        @pl.when(slot(level, number))
+        def _():
+            for gi in range(len(key_groups)):
+                key_step(gi)
+
+    def query_slot(number):
+        @pl.when(slot(back_level, number))
+        def _():
+            for gi in local:
+                query_step(gi)
+
     loads[3].wait()
     loads[4].wait()
+    project(g_own, 0, T, gat.at[0], [c])
     w_copy.wait_recv()
-    project(g_own, 0, T, gat.at[0])
+    project(g_own, 0, T, gat.at[0], [1 - c])
     loads[5].wait()
     loads[6].wait()
-    local = [gi for gi, g in enumerate(q_groups) if g[0] == 0]
-    distant = [gi for gi, g in enumerate(q_groups) if g[0] > 0]
     for gi in local:
         send_query_states(gi)
-    for gi in range(len(key_groups)):
-        key_step(gi)
+    key_slot(0)
 
     ret_copies = []
 
     def serve(i):
         for s in range(X - 1):
             grad_copies[i, s].wait_recv()
-            project(g_rem.at[s], i * R, R, ret.at[s])
+            project(g_rem.at[s], i * R, R, ret.at[s], [0, 1])
             back = X - 1 - s
             copy = remote(
                 ret.at[s, pl.ds(i * R, R), :], gat.at[back, pl.ds(i * R, R), :],
@@ -299,30 +325,45 @@
             ret_copies.append(copy)
 
     serve(0)
-    for gi in local:
-        query_step(gi)
+    query_slot(0)
+    serve(1)
     inside(0)
-    store(0, 0)
-    serve(1)
-    for gi in local:
-        across(*q_groups[gi])
-    store(1, 0)
-    store(2, 0)
+    key_slot(1)
+    query_slot(1)
     for i in range(2, NC):
         serve(i)
+    key_slot(2)
+    query_slot(2)
     for copy in ret_copies:
         copy.wait_recv()
     for gi in distant:
         send_query_states(gi)
+    query_slot(3)
     for j in range(1, X):
         inside(j)
-        store(0, j)
+    for gi in local:
+        across_q(*q_groups[gi])
+    store(1, 0)
+    store(2, 0)
+
+    @pl.when(level < 3)
+    def _():
+        across_k()
+
     for gi in distant:
         query_step(gi)
-        across(*q_groups[gi])
+        across_q(*q_groups[gi])
     for j in range(1, X):
         store(1, j)
         store(2, j)
+    key_slot(3)
+
+    @pl.when(level >= 3)
+    def _():
+        across_k()
+
+    for j in range(X):
+        store(0, j)
 
     for copy in list(grad_copies.values()) + [w_copy] + ret_copies + key_pair:
         copy.wait_send()
@@ -331,16 +372,32 @@
 
     @pl.when(has_hi)
     def _():
-        for copy in key_chain:
-            copy.wait_send()
+        for gi in range(len(key_groups)):
+            key_copy(gi)[1].wait_send()
 
     @pl.when(has_lo)
     def _():
-        for copy in query_chain:
-            copy.wait_send()
+        for gi in range(len(q_groups)):
+            query_copy(gi)[1].wait_send()
 
     for copy in outs:
         copy.wait()
+
+
+def settle(a, b, c, oa, ob, oc, buf, isem, osem):
+    rows = buf.shape[1] // 2
+    pairs = []
+    for o, (src, dst) in enumerate(((a, oa), (b, ob), (c, oc))):
+        for i in range(2):
+            part = pl.ds(i * rows, rows)
+            into = pltpu.make_async_copy(src.at[0, part], buf.at[o, part], isem.at[o, i])
+            into.start()
+            pairs.append((into, pltpu.make_async_copy(buf.at[o, part], dst.at[0, part], osem.at[o, i])))
+    for into, out in pairs:
+        into.wait()
+        out.start()
+    for _, out in pairs:
+        out.wait()
 
 
 def body(n_seq, n_dp, out_grad, w_out, queries, keys, values, keep_bits, query_later):
@@ -372,6 +429,7 @@
         state, state, state, state, state,
         pltpu.VMEM((H, T, HD), F32),
         pltpu.VMEM((H, T, HD), F32),
+        pltpu.VMEM((H, T, HD), F32),
         pltpu.VMEM((3, T, I), BF),
         dma((7,)), dma((2,)),
         dma((NC, far)), dma((NC, far)), dma((NC, far)), dma((NC, far)),
@@ -381,7 +439,7 @@
     ]
     out = jax.ShapeDtypeStruct((1, T, I), BF)
     hbm = pl.BlockSpec(memory_space=pl.ANY)
-    return pl.pallas_call(
+    parts = pl.pallas_call(
         functools.partial(kernel, n_seq, n_dp),
         out_shape=(out, out, out),
         in_specs=[hbm] * 7,
@@ -391,6 +449,13 @@
             collective_id=0, has_side_effects=True, vmem_limit_bytes=60 * 1024 * 1024
         ),
     )(out_grad, w_out, queries, keys, values, keep_bits, query_later)
+    return pl.pallas_call(
+        settle,
+        out_shape=(out, out, out),
+        in_specs=[hbm] * 3,
+        out_specs=(hbm, hbm, hbm),
+        scratch_shapes=[pltpu.VMEM((3, T, I), BF), dma((3, 2)), dma((3, 2))],
+    )(*parts)
 
 
 def solution(mesh):

time: 92.6 us -> 75 us (0.81)
  Pallas kernels: 85.5 us -> 74.3 us
  local copies, waits for them, and re-layouts: 6.26 us -> 0 us
    pallas_call x1, Pallas kernels: 85.5 us -> 71.8 us  [body(): pl.pallas_call(functools.partial(kernel, n_seq, n_dp), out_shape=(out, ou...]
    unnamed x3 -> x0, local copies, waits for them, and re-layouts: 6.26 us -> none
    pallas_call x0 -> x1, Pallas kernels: none -> 2.49 us  [body(): pl.pallas_call(settle, out_shape=(out, out, out), in_specs=[hbm] * 3, out...]
where the time goes in v2:
time: 75 us; the launch traced here: 74.9 us
  Pallas kernels  74.3 us (99%)
    pallas_call x1, Pallas kernels, body(): pl.pallas_call(functools.partial(kernel, n_seq, n_dp), out_shape=(out, ou...  71.8 us
    pallas_call x1, Pallas kernels, body(): pl.pallas_call(settle, out_shape=(out, out, out), in_specs=[hbm] * 3, out...  2.49 us

profile of v2, /device:TPU:0, one launch (start us, length us, event | category | flops | bytes accessed | tf_op | source)
XLA Modules:
  0.0 74.9 jit_solution(12301130610550867205)
XLA Ops:
  0.6 71.8 %shard_map.94 = (bf16[1,192,2048]{2,1,0:T(8,128)(2,1)}, bf16[1,192,2048]{2,1,0:T(8,128)(2,1)}, bf16[1,192,2048]{2,1,0:T(8,128)(2,1)}) custom-call(bf16[1,192,4096]{2,1,0:T(8,128)(2,1)} %og.1, bf16[512,4096]{1,0:T(8,128)(2,1)} %w.1, bf16[1,192,2048]{2,1,0:T(8,128)(2,1)} %q.1, bf16[1,192,2048]{2,1,0:T(8,128)(2,1)} %k.1, bf16[1,192,2048]{2,1,0:T(8,128)(2,1)} %v.1, ...), custom_call_target="tpu_custom_call" | custom-call | tf_op jit(solution)/shard_map/pallas_call | solution.py:442
  72.4 2.5 %shard_map.95 = (bf16[1,192,2048]{2,1,0:T(8,128)(2,1)}, bf16[1,192,2048]{2,1,0:T(8,128)(2,1)}, bf16[1,192,2048]{2,1,0:T(8,128)(2,1)}) custom-call(bf16[1,192,2048]{2,1,0:T(8,128)(2,1)} %get-tuple-element.6.a, bf16[1,192,2048]{2,1,0:T(8,128)(2,1)} %get-tuple-element.7.b, bf16[1,192,2048]{2,1,0:T(8,128)(2,1)} %get-tuple-element.8.c), custom_call_target="tpu_custom_call" | custom-call | tf_op jit(solution)/shard_map/pallas_call | solution.py:452

commit v3 on v2

--- a/solution.py
+++ b/solution.py
@@ -177,7 +177,7 @@
 
     q_groups = []
     for j in range(X):
-        for hl0, cnt in split(0, Hc, 4 if j == 0 else 2):
+        for hl0, cnt in split(0, Hc, 4 if j == 0 else 1):
             q_groups.append((j, hl0, cnt))
     query_pair = {}
 
@@ -239,9 +239,10 @@
         lax.broadcasted_iota(jnp.int32, (T, T), 0) >= lax.broadcasted_iota(jnp.int32, (T, T), 1)
     )
 
-    def inside(j):
-        @pl.loop(0, Hc)
-        def _(hl):
+    def inside(j, hl0, cnt):
+        @pl.loop(0, cnt)
+        def _(i):
+            hl = hl0 + i
             h = head_of(j, hl)
             p = j * Hc + hl
             g = gat[j, :, lanes(hl)]
@@ -310,47 +311,64 @@
         send_query_states(gi)
     key_slot(0)
 
-    ret_copies = []
+    ret_copies = ([], [])
+
+    def give_back(cc, i, s, row0, rows):
+        back = X - 1 - s
+        part = (pl.ds(row0, rows), pl.ds(cc * Wr, Wr))
+        copy = remote(
+            ret.at[(s, *part)], gat.at[(back, *part)],
+            rsend.at[cc, i, s], rrecv.at[cc, i, back - 1], far[s],
+        )
+        copy.start()
+        ret_copies[cc].append(copy)
 
     def serve(i):
         for s in range(X - 1):
             grad_copies[i, s].wait_recv()
-            project(g_rem.at[s], i * R, R, ret.at[s], [0, 1])
-            back = X - 1 - s
-            copy = remote(
-                ret.at[s, pl.ds(i * R, R), :], gat.at[back, pl.ds(i * R, R), :],
-                rsend.at[i, s], rrecv.at[i, back - 1], far[s],
-            )
-            copy.start()
-            ret_copies.append(copy)
-
+            project(g_rem.at[s], i * R, R, ret.at[s], [0])
+            give_back(0, i, s, i * R, R)
+            if i == NC - 1:
+                give_back(1, 0, s, 0, i * R)
+            project(g_rem.at[s], i * R, R, ret.at[s], [1])
+            if i == NC - 1:
+                give_back(1, 1, s, i * R, R)
+
+    half = Hc // 2
+    distant = [[gi for gi in distant if (q_groups[gi][1] >= half) == late] for late in (False, True)]
     serve(0)
     query_slot(0)
     serve(1)
-    inside(0)
+    inside(0, 0, Hc)
     key_slot(1)
     query_slot(1)
     for i in range(2, NC):
         serve(i)
     key_slot(2)
     query_slot(2)
-    for copy in ret_copies:
+    for copy in ret_copies[0]:
         copy.wait_recv()
-    for gi in distant:
+    for gi in distant[0]:
         send_query_states(gi)
     query_slot(3)
     for j in range(1, X):
-        inside(j)
+        inside(j, 0, half)
     for gi in local:
         across_q(*q_groups[gi])
     store(1, 0)
     store(2, 0)
+    for copy in ret_copies[1]:
+        copy.wait_recv()
+    for gi in distant[1]:
+        send_query_states(gi)
+    for j in range(1, X):
+        inside(j, half, Hc - half)
 
     @pl.when(level < 3)
     def _():
         across_k()
 
-    for gi in distant:
+    for gi in distant[0] + distant[1]:
         query_step(gi)
         across_q(*q_groups[gi])
     for j in range(1, X):
@@ -365,7 +383,7 @@
     for j in range(X):
         store(0, j)
 
-    for copy in list(grad_copies.values()) + [w_copy] + ret_copies + key_pair:
+    for copy in list(grad_copies.values()) + [w_copy] + ret_copies[0] + ret_copies[1] + key_pair:
         copy.wait_send()
     for copy in query_pair.values():
         copy.wait_send()
@@ -409,7 +427,7 @@
     X = n_dp // 2
     H = I // HD
     kgn = len(split(0, H, 4))
-    qgn = len(split(0, Hc, 4)) + (X - 1) * len(split(0, Hc, 2))
+    qgn = len(split(0, Hc, 4)) + (X - 1) * len(split(0, Hc, 1))
     state = pltpu.VMEM((H, HD, HD), BF)
     dma = pltpu.SemaphoreType.DMA
     far = max(X - 1, 1)
@@ -432,7 +450,7 @@
         pltpu.VMEM((H, T, HD), F32),
         pltpu.VMEM((3, T, I), BF),
         dma((7,)), dma((2,)),
-        dma((NC, far)), dma((NC, far)), dma((NC, far)), dma((NC, far)),
+        dma((NC, far)), dma((NC, far)), dma((2, NC, far)), dma((2, NC, far)),
         dma((kgn,)), dma((kgn,)), dma((kgn,)), dma((kgn,)),
         dma((qgn,)), dma((qgn,)), dma((qgn,)), dma((qgn,)),
         dma((3, X)),

time: 75 us -> 70.1 us (0.935)
  Pallas kernels: 74.3 us -> 69.4 us
    pallas_call x1, Pallas kernels: 71.8 us -> 66.9 us  [body(): pl.pallas_call(functools.partial(kernel, n_seq, n_dp), out_shape=(out, ou...]
where the time goes in v3:
time: 70.1 us; the launch traced here: 70 us
  Pallas kernels  69.4 us (99%)
    pallas_call x1, Pallas kernels, body(): pl.pallas_call(functools.partial(kernel, n_seq, n_dp), out_shape=(out, ou...  66.9 us
    pallas_call x1, Pallas kernels, body(): pl.pallas_call(settle, out_shape=(out, out, out), in_specs=[hbm] * 3, out...  2.49 us

profile of v3, /device:TPU:0, one launch (start us, length us, event | category | flops | bytes accessed | tf_op | source)
XLA Modules:
  0.0 70.0 jit_solution(4116038309752378154)
XLA Ops:
  0.6 66.9 %shard_map.94 = (bf16[1,192,2048]{2,1,0:T(8,128)(2,1)}, bf16[1,192,2048]{2,1,0:T(8,128)(2,1)}, bf16[1,192,2048]{2,1,0:T(8,128)(2,1)}) custom-call(bf16[1,192,4096]{2,1,0:T(8,128)(2,1)} %og.1, bf16[512,4096]{1,0:T(8,128)(2,1)} %w.1, bf16[1,192,2048]{2,1,0:T(8,128)(2,1)} %q.1, bf16[1,192,2048]{2,1,0:T(8,128)(2,1)} %k.1, bf16[1,192,2048]{2,1,0:T(8,128)(2,1)} %v.1, ...), custom_call_target="tpu_custom_call" | custom-call | tf_op jit(solution)/shard_map/pallas_call | solution.py:460
  67.5 2.5 %shard_map.95 = (bf16[1,192,2048]{2,1,0:T(8,128)(2,1)}, bf16[1,192,2048]{2,1,0:T(8,128)(2,1)}, bf16[1,192,2048]{2,1,0:T(8,128)(2,1)}) custom-call(bf16[1,192,2048]{2,1,0:T(8,128)(2,1)} %get-tuple-element.6.a, bf16[1,192,2048]{2,1,0:T(8,128)(2,1)} %get-tuple-element.7.b, bf16[1,192,2048]{2,1,0:T(8,128)(2,1)} %get-tuple-element.8.c), custom_call_target="tpu_custom_call" | custom-call | tf_op jit(solution)/shard_map/pallas_call | solution.py:470
